TPU v7x, 32 devices: a whole 2x2x4 slice. The times are simulated.
32 devices in a mesh: exp: 8 (over z, x), rep: 4 (over y, core).
Axes of the slice: x: 2, y: 2, z: 4, core: 2. Of those that a mesh axis runs over, the one named last changes fastest.
Arguments:
- tokens: bfloat16 [18432, 768], P(('exp', 'rep')), may hold values from -6 to 6
- ln1_gain: bfloat16 [768], P(('exp', 'rep')), may hold values from 0.3984375 to 1.59375
- ln1_bias: bfloat16 [768], P(('exp', 'rep')), may hold values from -1.1953125 to 1.1953125
- w_qkv: bfloat16 [768, 2304], P(('exp', 'rep')), may hold values from -0.21875 to 0.21875
- w_out: bfloat16 [768, 768], P(('exp', 'rep')), may hold values from -2.5 to 2.5
- ln2_gain: bfloat16 [768], P(('exp', 'rep')), may hold values from 0.3984375 to 1.59375
- ln2_bias: bfloat16 [768], P(('exp', 'rep')), may hold values from -0.59765625 to 0.59765625
- w_router: bfloat16 [768, 8], P(('exp', 'rep')), may hold values from -0.109375 to 0.109375
- w_in: bfloat16 [8, 768, 3072], P('exp'), may hold values from -0.21875 to 0.21875
- b_in: bfloat16 [8, 3072], P('exp'), may hold values from -1.796875 to 1.796875
- w_back: bfloat16 [8, 3072, 768], P('exp'), may hold values from -0.625 to 0.625
- b_back: bfloat16 [8, 768], P('exp'), may hold values from -2.390625 to 2.390625
- lengths: int32 [32, 3], P(('exp', 'rep')), may hold values from 1 to 400, 576 in all within a row
- routes: int32 [18432, 2], P(('exp', 'rep')), may hold values from 0 to 7, all different within a row
- priority: int32 [18432], P(('exp', 'rep')), may hold values from 0 to 575, as said below
- padding: int32 [18432], P(('exp', 'rep')), may hold values 0 or 1
- cotangent: bfloat16 [18432, 768], P(('exp', 'rep')), may hold values from -6 to 6
Outputs:
- output: bfloat16 [18432, 768], P(('exp', 'rep'))
- grad_tokens: float32 [18432, 768], P(('exp', 'rep'))
- grad_ln1_gain: float32 [768], P(('exp', 'rep'))
- grad_ln1_bias: float32 [768], P(('exp', 'rep'))
- grad_w_qkv: float32 [768, 2304], P(('exp', 'rep'))
- grad_w_out: float32 [768, 768], P(('exp', 'rep'))
- grad_ln2_gain: float32 [768], P(('exp', 'rep'))
- grad_ln2_bias: float32 [768], P(('exp', 'rep'))
- grad_w_router: float32 [768, 8], P(('exp', 'rep'))
- grad_w_in: float32 [8, 768, 3072], P('exp')
- grad_b_in: float32 [8, 3072], P('exp')
- grad_w_back: float32 [8, 3072, 768], P('exp')
- grad_b_back: float32 [8, 768], P('exp')
Inputs may be any that keep to these rules, and one draw needn't show every extreme that they name: `routes`: each row names two different experts. `priority`: in each aligned group of 576 patches every value 0 to 575 appears once. `lengths`: each row sums to 576; its largest entry is 400.
All inputs are finite; a program needn't handle non-finite values. No bound on the sum of `padding` on one device may be relied on, other than what follows from the above.
Results may differ from a plain program's by a relative error of at most 0.014.
Values may be sent and summed in bfloat16 or wider, within the bound.
A program may use at most 192 MiB of HBM per device.

v0:
```python
import jax
import jax.numpy as jnp
from jax import lax
from jax.sharding import PartitionSpec as P

D = 768
HEADS = 12
HEAD = 64
SLOTS = 576
ROWS_DEV = 1
TOK_DEV = 576
root_half = 0.7071067811865476
inverse_root_tau = 0.3989422804014327
contract_first = (((0,), (0,)), ((), ()))
contract_last = (((1,), (1,)), ((), ()))


def norm_forward(inputs, gain, offset):
    center = inputs - jnp.mean(inputs, axis=-1, keepdims=True)
    inverse = lax.rsqrt(jnp.mean(center * center, axis=-1, keepdims=True) + 1e-06)
    normal = center * inverse
    return (normal * gain.astype(jnp.float32) + offset.astype(jnp.float32), normal, inverse)


def norm_backward(grad, normal, inverse, gain):
    scaled = grad * gain.astype(jnp.float32)
    grad_in = inverse * (
        scaled
        - jnp.mean(scaled, axis=-1, keepdims=True)
        - normal * jnp.mean(scaled * normal, axis=-1, keepdims=True)
    )
    return (grad_in, jnp.sum(grad * normal, axis=0), jnp.sum(grad, axis=0))


def gelu_slope(pre):
    return 0.5 * (1.0 + lax.erf(pre * root_half)) + pre * inverse_root_tau * jnp.exp(
        -0.5 * pre * pre
    )


def row_masks(lengths, padding):
    bounds = jnp.cumsum(lengths, axis=1)
    places = jnp.arange(SLOTS, dtype=jnp.int32)
    segments = jnp.sum((places[None, :, None] >= bounds[:, None, :]).astype(jnp.int32), axis=2)
    live = padding.reshape(ROWS_DEV, SLOTS) == 1
    same = segments[:, :, None] == segments[:, None, :]
    diagonal = places[:, None] == places[None, :]
    return same & (live[:, None, :] | diagonal[None])


def split_heads(qkv_row):
    query = qkv_row[:, :D].reshape(SLOTS, HEADS, HEAD)
    keys = qkv_row[:, D : 2 * D].reshape(SLOTS, HEADS, HEAD)
    values = qkv_row[:, 2 * D :].reshape(SLOTS, HEADS, HEAD)
    return (query, keys, values)


def masked_scores(query, keys, allowed_row):
    scores = jnp.einsum("qhc,khc->hqk", query, keys, preferred_element_type=jnp.float32) * HEAD ** (
        -0.5
    )
    return jnp.where(allowed_row[None], scores, -1e30)


def attend_forward(qkv_row, allowed_row):
    query, keys, values = split_heads(qkv_row)
    scores = masked_scores(query, keys, allowed_row)
    top = jnp.max(scores, axis=-1, keepdims=True)
    expo = jnp.exp(scores - top)
    total = jnp.sum(expo, axis=-1, keepdims=True)
    probs = (expo / total).astype(jnp.bfloat16)
    mixed = jnp.einsum("hqk,khc->qhc", probs, values, preferred_element_type=jnp.float32)
    return (mixed.reshape(SLOTS, D), top + jnp.log(total))


def attend_backward(qkv_row, allowed_row, lse_row, grad_row):
    query, keys, values = split_heads(qkv_row)
    probs = jnp.exp(masked_scores(query, keys, allowed_row) - lse_row)
    grad_mixed = grad_row.reshape(SLOTS, HEADS, HEAD)
    grad_probs = jnp.einsum("qhc,khc->hqk", grad_mixed, values, preferred_element_type=jnp.float32)
    grad_values = jnp.einsum(
        "hqk,qhc->khc", probs.astype(jnp.bfloat16), grad_mixed, preferred_element_type=jnp.float32
    )
    grad_scores = (
        probs * (grad_probs - jnp.sum(probs * grad_probs, axis=-1, keepdims=True))
    ).astype(jnp.bfloat16)
    grad_query = jnp.einsum(
        "hqk,khc->qhc", grad_scores, keys, preferred_element_type=jnp.float32
    ) * HEAD ** (-0.5)
    grad_keys = jnp.einsum(
        "hqk,qhc->khc", grad_scores, query, preferred_element_type=jnp.float32
    ) * HEAD ** (-0.5)
    joined = jnp.concatenate(
        [grad_query.reshape(SLOTS, D), grad_keys.reshape(SLOTS, D), grad_values.reshape(SLOTS, D)],
        axis=1,
    )
    return joined.astype(jnp.bfloat16)


def dispatch_tables(routes, priority, padding, experts, capacity):
    labels = jnp.arange(experts, dtype=jnp.int32)
    first_hot = (routes[:, 0:1] == labels[None, :]).astype(jnp.bfloat16)
    second_hot = (routes[:, 1:2] == labels[None, :]).astype(jnp.bfloat16)
    live = padding[:, None].astype(jnp.bfloat16)
    earlier = (priority[None, :] < priority[:, None]).astype(jnp.bfloat16)
    before_first = jnp.dot(earlier, first_hot * live, preferred_element_type=jnp.float32)
    first_counts = jnp.sum((first_hot * live).astype(jnp.float32), axis=0)
    before_second = (
        jnp.dot(earlier, second_hot * live, preferred_element_type=jnp.float32)
        + first_counts[None, :]
    )
    place_first = jnp.sum(before_first * first_hot, axis=1).astype(jnp.int32)
    place_second = jnp.sum(before_second * second_hot, axis=1).astype(jnp.int32)
    kept_first = (padding == 1) & (place_first < capacity)
    kept_second = (padding == 1) & (place_second < capacity)
    slot_labels = jnp.arange(experts * capacity, dtype=jnp.int32)
    slot_first = routes[:, 0] * capacity + place_first
    slot_second = routes[:, 1] * capacity + place_second
    pick_first = ((slot_first[:, None] == slot_labels[None, :]) & kept_first[:, None]).astype(
        jnp.bfloat16
    )
    pick_second = ((slot_second[:, None] == slot_labels[None, :]) & kept_second[:, None]).astype(
        jnp.bfloat16
    )
    return (first_hot.astype(jnp.float32), second_hot.astype(jnp.float32), pick_first, pick_second)


def on_device(
    tokens,
    ln1_gain,
    ln1_bias,
    w_qkv,
    w_out,
    ln2_gain,
    ln2_bias,
    w_router,
    w_in,
    b_in,
    w_back,
    b_back,
    lengths,
    routes,
    priority,
    padding,
    cotangent,
):
    experts = lax.axis_size("exp")
    capacity = (TOK_DEV * 210 + experts * 100 - 1) // (experts * 100)
    dense = (
        lax.all_gather(ln1_gain, ("exp", "rep"), axis=0, tiled=True),
        lax.all_gather(ln1_bias, ("exp", "rep"), axis=0, tiled=True),
        lax.all_gather(w_qkv, ("exp", "rep"), axis=0, tiled=True),
        lax.all_gather(w_out, ("exp", "rep"), axis=0, tiled=True),
        lax.all_gather(ln2_gain, ("exp", "rep"), axis=0, tiled=True),
        lax.all_gather(ln2_bias, ("exp", "rep"), axis=0, tiled=True),
        lax.all_gather(w_router, ("exp", "rep"), axis=0, tiled=True),
    )
    gain_one, bias_one, qkv_weight, out_weight, gain_two, bias_two, router_weight = dense
    inputs = tokens.astype(jnp.float32)
    normed, normal_one, inverse_one = norm_forward(inputs, gain_one, bias_one)
    normed_low = normed.astype(jnp.bfloat16)
    qkv = (
        jnp.dot(normed_low, qkv_weight, preferred_element_type=jnp.float32)
        .astype(jnp.bfloat16)
        .reshape(ROWS_DEV, SLOTS, 3 * D)
    )
    allowed = row_masks(lengths, padding)
    mixed, lse = lax.map(lambda pair: attend_forward(pair[0], pair[1]), (qkv, allowed))
    mixed_low = mixed.reshape(TOK_DEV, D).astype(jnp.bfloat16)
    resid = inputs + jnp.dot(mixed_low, out_weight, preferred_element_type=jnp.float32)
    routed_float, normal_two, inverse_two = norm_forward(resid, gain_two, bias_two)
    routed = routed_float.astype(jnp.bfloat16)
    logits = jnp.dot(routed, router_weight, preferred_element_type=jnp.float32)
    probs = jax.nn.softmax(logits, axis=-1)
    first_hot, second_hot, pick_first, pick_second = dispatch_tables(
        routes, priority, padding, experts, capacity
    )
    picks = pick_first + pick_second
    buffer = lax.dot_general(picks, routed, contract_first, preferred_element_type=jnp.float32)
    buffer = buffer.astype(jnp.bfloat16).reshape(experts, capacity, D)
    received_part = lax.all_to_all(buffer, "exp", split_axis=0, concat_axis=0, tiled=True)
    pre_part = jnp.einsum(
        "scd,df->scf", received_part, w_in[0], preferred_element_type=jnp.float32
    ) + b_in[0].astype(jnp.float32)
    active_part = jax.nn.gelu(pre_part, approximate=False).astype(jnp.bfloat16)
    result_part = jnp.einsum(
        "scf,fd->scd", active_part, w_back[0], preferred_element_type=jnp.float32
    ) + b_back[0].astype(jnp.float32)
    returned = lax.all_to_all(
        result_part.astype(jnp.bfloat16), "exp", split_axis=0, concat_axis=0, tiled=True
    )
    returned_flat = returned.reshape(experts * capacity, D)
    picked_first = jnp.dot(pick_first, returned_flat, preferred_element_type=jnp.float32)
    picked_second = jnp.dot(pick_second, returned_flat, preferred_element_type=jnp.float32)
    gate_first = jnp.sum(probs * first_hot, axis=1)
    gate_second = jnp.sum(probs * second_hot, axis=1)
    output = resid + gate_first[:, None] * picked_first + gate_second[:, None] * picked_second
    grad_out = cotangent.astype(jnp.float32)
    gated_first = (gate_first[:, None] * grad_out).astype(jnp.bfloat16)
    gated_second = (gate_second[:, None] * grad_out).astype(jnp.bfloat16)
    grad_slots = lax.dot_general(
        pick_first, gated_first, contract_first, preferred_element_type=jnp.float32
    )
    grad_slots = grad_slots + lax.dot_general(
        pick_second, gated_second, contract_first, preferred_element_type=jnp.float32
    )
    grad_results = lax.all_to_all(
        grad_slots.astype(jnp.bfloat16).reshape(experts, capacity, D),
        "exp",
        split_axis=0,
        concat_axis=0,
        tiled=True,
    )
    pre = jnp.einsum(
        "scd,df->scf", received_part, w_in[0], preferred_element_type=jnp.float32
    ) + b_in[0].astype(jnp.float32)
    active = jax.nn.gelu(pre, approximate=False).astype(jnp.bfloat16)
    grad_w_back = jnp.einsum(
        "scf,scd->fd", active, grad_results, preferred_element_type=jnp.float32
    )
    grad_b_back = jnp.sum(grad_results.astype(jnp.float32), axis=(0, 1))
    grad_active = jnp.einsum(
        "scd,fd->scf", grad_results, w_back[0], preferred_element_type=jnp.float32
    )
    grad_pre = (grad_active * gelu_slope(pre)).astype(jnp.bfloat16)
    grad_w_in = jnp.einsum(
        "scd,scf->df", received_part, grad_pre, preferred_element_type=jnp.float32
    )
    grad_b_in = jnp.sum(grad_pre.astype(jnp.float32), axis=(0, 1))
    expert_sums = (
        lax.psum(grad_w_in.astype(jnp.bfloat16), "rep").astype(jnp.float32),
        lax.psum(grad_b_in.astype(jnp.bfloat16), "rep").astype(jnp.float32),
        lax.psum(grad_w_back.astype(jnp.bfloat16), "rep").astype(jnp.float32),
        lax.psum(grad_b_back.astype(jnp.bfloat16), "rep").astype(jnp.float32),
    )
    grad_received = jnp.einsum(
        "scf,df->scd", grad_pre, w_in[0], preferred_element_type=jnp.float32
    ).astype(jnp.bfloat16)
    grad_buffer = lax.all_to_all(
        grad_received, "exp", split_axis=0, concat_axis=0, tiled=True
    ).reshape(experts * capacity, D)
    grad_gate_first = jnp.sum(grad_out * picked_first, axis=1)
    grad_gate_second = jnp.sum(grad_out * picked_second, axis=1)
    grad_probs = grad_gate_first[:, None] * first_hot + grad_gate_second[:, None] * second_hot
    grad_logits = (
        probs * (grad_probs - jnp.sum(probs * grad_probs, axis=1, keepdims=True))
    ).astype(jnp.bfloat16)
    dense_back = (
        lax.all_gather(ln1_gain, ("exp", "rep"), axis=0, tiled=True),
        lax.all_gather(ln1_bias, ("exp", "rep"), axis=0, tiled=True),
        lax.all_gather(w_qkv, ("exp", "rep"), axis=0, tiled=True),
        lax.all_gather(w_out, ("exp", "rep"), axis=0, tiled=True),
        lax.all_gather(ln2_gain, ("exp", "rep"), axis=0, tiled=True),
        lax.all_gather(ln2_bias, ("exp", "rep"), axis=0, tiled=True),
        lax.all_gather(w_router, ("exp", "rep"), axis=0, tiled=True),
    )
    gain_one, bias_one, qkv_weight, out_weight, gain_two, bias_two, router_weight = dense_back
    grad_router = lax.dot_general(
        routed, grad_logits, contract_first, preferred_element_type=jnp.float32
    )
    grad_routed = jnp.dot(picks, grad_buffer, preferred_element_type=jnp.float32)
    grad_routed = grad_routed + lax.dot_general(
        grad_logits, router_weight, contract_last, preferred_element_type=jnp.float32
    )
    grad_norm_two, grad_gain_two, grad_bias_two = norm_backward(
        grad_routed, normal_two, inverse_two, gain_two
    )
    grad_resid = grad_out + grad_norm_two
    grad_attn = grad_resid.astype(jnp.bfloat16)
    grad_out_weight = lax.dot_general(
        mixed_low, grad_attn, contract_first, preferred_element_type=jnp.float32
    )
    grad_mixed = lax.dot_general(
        grad_attn, out_weight, contract_last, preferred_element_type=jnp.float32
    )
    grad_mixed = grad_mixed.astype(jnp.bfloat16).reshape(ROWS_DEV, SLOTS, D)
    grad_qkv = lax.map(
        lambda group: attend_backward(group[0], group[1], group[2], group[3]),
        (qkv, allowed, lse, grad_mixed),
    )
    grad_qkv = grad_qkv.reshape(TOK_DEV, 3 * D)
    grad_qkv_weight = lax.dot_general(
        normed_low, grad_qkv, contract_first, preferred_element_type=jnp.float32
    )
    grad_normed = lax.dot_general(
        grad_qkv, qkv_weight, contract_last, preferred_element_type=jnp.float32
    )
    grad_norm_one, grad_gain_one, grad_bias_one = norm_backward(
        grad_normed, normal_one, inverse_one, gain_one
    )
    grad_tokens = grad_resid + grad_norm_one
    dense_grads = (
        lax.psum_scatter(grad_gain_one, ("exp", "rep"), scatter_dimension=0, tiled=True),
        lax.psum_scatter(grad_bias_one, ("exp", "rep"), scatter_dimension=0, tiled=True),
        lax.psum_scatter(grad_qkv_weight, ("exp", "rep"), scatter_dimension=0, tiled=True),
        lax.psum_scatter(grad_out_weight, ("exp", "rep"), scatter_dimension=0, tiled=True),
        lax.psum_scatter(grad_gain_two, ("exp", "rep"), scatter_dimension=0, tiled=True),
        lax.psum_scatter(grad_bias_two, ("exp", "rep"), scatter_dimension=0, tiled=True),
        lax.psum_scatter(grad_router, ("exp", "rep"), scatter_dimension=0, tiled=True),
    )
    return (
        output.astype(jnp.bfloat16),
        grad_tokens,
        dense_grads[0],
        dense_grads[1],
        dense_grads[2],
        dense_grads[3],
        dense_grads[4],
        dense_grads[5],
        dense_grads[6],
        expert_sums[0][None],
        expert_sums[1][None],
        expert_sums[2][None],
        expert_sums[3][None],
    )


def solution(mesh):
    return jax.shard_map(
        on_device,
        mesh=mesh,
        in_specs=(
            P(("exp", "rep"), None),
            P(("exp", "rep")),
            P(("exp", "rep")),
            P(("exp", "rep"), None),
            P(("exp", "rep"), None),
            P(("exp", "rep")),
            P(("exp", "rep")),
            P(("exp", "rep"), None),
            P("exp", None, None),
            P("exp", None),
            P("exp", None, None),
            P("exp", None),
            P(("exp", "rep"), None),
            P(("exp", "rep"), None),
            P(("exp", "rep")),
            P(("exp", "rep")),
            P(("exp", "rep"), None),
        ),
        out_specs=(
            P(("exp", "rep"), None),
            P(("exp", "rep"), None),
            P(("exp", "rep")),
            P(("exp", "rep")),
            P(("exp", "rep"), None),
            P(("exp", "rep"), None),
            P(("exp", "rep")),
            P(("exp", "rep")),
            P(("exp", "rep"), None),
            P("exp", None, None),
            P("exp", None),
            P("exp", None, None),
            P("exp", None),
        ),
        check_vma=False,
    )
```

profile of v0, /device:TPU:0, one launch (start us, length us, event | category | flops | bytes accessed | tf_op | source)
XLA Modules:
  0.0 835.7 jit_solution(4616695605341948638)
XLA Ops:
  10.2 1.2 fusion.102
  12.1 0.8 dynamic-update-slice.3
  13.0 0.8 dynamic-update-slice
  13.8 0.8 dynamic-update-slice.1
  14.6 0.8 dynamic-update-slice.2
  15.5 42.2 %all-reduce.10 = (bf16[768]{0:T(1024)(128)(2,1)S(1)}, bf16[768]{0:T(1024)(128)(2,1)S(1)}, bf16[768]{0:T(1024)(128)(2,1)S(1)}, bf16[768]{0:T(1024)(128)(2,1)S(1)}) all-reduce(bf16[768]{0:T(1024)(128)(2,1)S(1)} %dynamic-update-slice.1, bf16[768]{0:T(1024)(128)(2,1)S(1)} %dynamic-update-slice, ...), channel_id=1, replica_groups=mesh['exp'=8,'rep'=4] {'exp','rep'}, use_global_device_ids=true, to_apply=%add.1 | all-reduce | flops 3072 | bytes 12288
  58.6 1.4 convert_reduce_fusion
  60.0 1.6 fusion.65
  62.4 1.2 fusion.99
  64.7 9.0 %all-gather.4.cloned.1.call-done = bf16[768,2304]{1,0:T(8,128)(2,1)} async-done(((bf16[24,2304]{1,0:T(8,128)(2,1)}), bf16[768,2304]{1,0:T(8,128)(2,1)}) %all-gather.4.cloned.1.call-update) | async-done | bytes 3538960 | tf_op jit(solution)/shard_map/all_gather | solution.py:152
  73.7 4.7 convolution_convert_fusion
  78.4 1.1 fusion.140
  80.1 1.9 copy.61
  82.0 1.4 copy.60
  83.4 8.0 fusion.141
  91.4 8.6 %fusion = f32[12,576]{1,0:T(8,128)S(1)} fusion(f32[12,576,576]{1,2,0:T(8,128)} %get-tuple-element.84, f32[12,576]{1,0:T(8,128)S(1)} %get-tuple-element.83), kind=kLoop, calls=%fused_computation.8 | loop fusion | flops 7955712 | bytes 15980544 | tf_op jit(solution)/shard_map/while/body/eval_jaxpr/reduce_sum | solution.py:70
  100.0 10.3 %fusion.81 = bf16[12,64,576]{2,1,0:T(8,128)(2,1)} fusion(bf16[576,12,64]{0,2,1:T(8,128)(2,1)S(1)} %bitcast.102, f32[12,576,576]{1,2,0:T(8,128)} %get-tuple-element.84, f32[12,576]{1,0:T(8,128)S(1)} %fusion, f32[12,576]{1,0:T(8,128)S(1)} %get-tuple-element.83), kind=kOutput, calls=%fused_computation.121 | convolution fusion | flops 521994240 | bytes 17750016 | tf_op jit(solution)/shard_map/while/body/eval_jaxpr/hqk,khc->qhc/dot_general | solution.py:72
  110.3 19.1 %all-gather.6.cloned.1.call-done = bf16[768,768]{1,0:T(8,128)(2,1)} async-done(((bf16[24,768]{1,0:T(8,128)(2,1)}), bf16[768,768]{1,0:T(8,128)(2,1)}) %all-gather.6.cloned.1.call-update) | async-done | bytes 1179664 | tf_op jit(solution)/shard_map/all_gather | solution.py:153
  129.4 2.6 fusion.142
  132.7 3.5 convolution_convert_fusion.1
  136.2 5.1 all-to-all-start
  141.4 43.8 %all-to-all-done = bf16[8,152,768]{2,1,0:T(8,128)(2,1)} async-done(((bf16[8,152,768]{2,1,0:T(8,128)(2,1)}), bf16[8,152,768]{2,1,0:T(8,128)(2,1)}, u32[]{:S(2)}, u32[]{:S(2)}) %all-to-all-start) | async-done | bytes 1867808 | tf_op jit(solution)/shard_map/all_to_all | solution.py:181
  185.1 12.7 %fusion.30 = (u8[152,3072]{1,0:T(8,128)(4,1)S(1)}, u8[152,3072]{1,0:T(8,128)(4,1)S(1)}, f32[8,152,3072]{2,1,0:T(8,128)S(1)}) fusion(f32[3072]{0:T(1024)S(1)} %bitcast.113, bf16[8,152,768]{2,1,0:T(8,128)(2,1)} %all-to-all-done, bf16[1,768,3072]{2,1,0:T(8,128)(2,1)} %param.25), kind=kOutput, calls=%fused_computation.54 | convolution fusion | flops 5789171712 | bytes 22474752 | tf_op jit(solution)/shard_map/scd,df->scf/dot_general | solution.py:182
  197.9 34.1 %fusion.3 = bf16[8,152,3072]{2,1,0:T(8,128)(2,1)S(1)} fusion(f32[8,152,3072]{2,1,0:T(8,128)S(1)} %get-tuple-element.87, f32[3072]{0:T(1024)S(1)} %bitcast.114, u8[152,3072]{1,0:T(8,128)(4,1)S(1)} %get-tuple-element.47, u8[152,3072]{1,0:T(8,128)(4,1)S(1)} %get-tuple-element.46), kind=kLoop, calls=%fused_computation.11 | loop fusion | flops 265224192 | bytes 23359488 | tf_op jit(solution)/shard_map/convert_element_type | solution.py:185
  232.0 3.1 copy-done.10
  235.1 9.4 %add_convert_fusion = bf16[8,152,768]{2,1,0:T(8,128)(2,1)} fusion(f32[768]{0:T(1024)S(1)} %convert_reduce_fusion.2, bf16[8,152,3072]{2,1,0:T(8,128)(2,1)S(1)} %fusion.3, bf16[1,3072,768]{2,1,0:T(8,128)(2,1)} %param.27), kind=kOutput, calls=%fused_computation.52 | convolution fusion | flops 5739675648 | bytes 14060544 | tf_op jit(solution)/shard_map/scf,fd->scd/dot_general | solution.py:186
  244.5 4.4 all-to-all-start.1
  249.0 65.3 %all-gather = bf16[32,24,8]{1,2,0:T(8,128)(2,1)S(1)} all-gather(bf16[1,24,8]{1,2,0:T(8,128)(2,1)S(1)} %bitcast.116), channel_id=1, replica_groups=mesh['exp'=8,'rep'=4] {'exp','rep'}, dimensions={0}, use_global_device_ids=true | all-gather | bytes 12672 | tf_op jit(solution)/shard_map/all_gather | solution.py:156
  314.9 3.1 fusion.40
  318.0 5.0 fusion.68
  323.1 2.1 fusion.33
  325.2 2.2 fusion.31
  327.5 50.3 %all_to_all.20 = bf16[8,152,768]{2,1,0:T(8,128)(2,1)S(1)} all-to-all(bf16[8,152,768]{2,1,0:T(8,128)(2,1)S(1)} %bitcast.106), channel_id=1, replica_groups=mesh['exp'=8,'rep'=4] {'exp'}, dimensions={0} | all-to-all | bytes 3735552 | tf_op jit(solution)/shard_map/all_to_all | solution.py:207
  377.9 12.3 %fusion.144 = (bf16[3072]{0:T(1024)(128)(2,1)}, bf16[8,152,3072]{2,1,0:T(8,128)(2,1)}) fusion(f32[8,152,3072]{2,1,0:T(8,128)S(1)} %bitcast.94, f32[3072]{0:T(1024)S(1)} %bitcast.115, bf16[8,152,768]{2,1,0:T(8,128)(2,1)S(1)} %all_to_all.20, bf16[1,3072,768]{2,1,0:T(8,128)(2,1)S(1)} %bitcast.119), kind=kOutput, calls=%fused_computation.194 | convolution fusion | flops 5782631424 | bytes 29018112 | tf_op jit(solution)/shard_map/scd,fd->scf/dot_general | solution.py:222
  390.2 10.7 %fusion.55 = bf16[8,152,768]{2,1,0:T(8,128)(2,1)} fusion(bf16[8,152,3072]{2,1,0:T(8,128)(2,1)} %get-tuple-element.96, bf16[1,768,3072]{2,1,0:T(8,128)(2,1)} %param.25), kind=kOutput, calls=%fused_computation.87 | convolution fusion | flops 5738741760 | bytes 14057472 | tf_op jit(solution)/shard_map/scf,df->scd/dot_general | solution.py:236
  400.9 4.3 all-to-all-start.3
  405.5 10.7 %fusion.28 = bf16[1,3072,768]{2,1,0:T(8,128)(2,1)} fusion(bf16[8,152,3072]{2,1,0:T(8,128)(2,1)} %copy-done.10, bf16[8,152,768]{2,1,0:T(8,128)(2,1)} %copy-done.11), kind=kOutput, calls=%fused_computation.50 | convolution fusion | flops 5740167168 | bytes 14057472 | tf_op jit(solution)/shard_map/scf,scd->fd/dot_general | solution.py:218
  416.2 10.6 %fusion.27 = bf16[1,768,3072]{2,1,0:T(8,128)(2,1)} fusion(bf16[8,152,768]{2,1,0:T(8,128)(2,1)} %all-to-all-done, bf16[8,152,3072]{2,1,0:T(8,128)(2,1)} %get-tuple-element.96), kind=kOutput, calls=%fused_computation.49 | convolution fusion | flops 5740167168 | bytes 14057472 | tf_op jit(solution)/shard_map/scd,scf->df/dot_general | solution.py:226
  427.5 20.3 %all-to-all-done.3 = bf16[8,152,768]{2,1,0:T(8,128)(2,1)} async-done(((bf16[8,152,768]{2,1,0:T(8,128)(2,1)}), bf16[8,152,768]{2,1,0:T(8,128)(2,1)}, u32[]{:S(2)}, u32[]{:S(2)}) %all-to-all-start.3) | async-done | bytes 1867808 | tf_op jit(solution)/shard_map/all_to_all | solution.py:239
  447.7 3.6 fusion.85
  451.4 1.6 multiply_reduce_fusion.1
  453.7 2.8 convert_add_fusion
  456.4 1.8 convolution_convert_fusion.2
  458.3 1.5 copy.65
  459.8 3.7 fusion.113
  464.1 12.5 %multiply_reduce_fusion = (f32[12,576]{1,0:T(8,128)S(1)}, f32[12,576,576]{1,2,0:T(8,128)}) fusion(f32[12,576,576]{1,2,0:T(8,128)} %get-tuple-element.84, f32[12,576]{1,0:T(8,128)S(1)} %copy-done.22, bf16[576,12,64]{0,2,1:T(8,128)(2,1)S(1)} %bitcast.97, bf16[576,12,64]{0,2,1:T(8,128)(2,1)} %bitcast.101), kind=kOutput, calls=%fused_computation.3 | convolution fusion | flops 521544960 | bytes 33675264 | tf_op jit(solution)/shard_map/while/body/eval_jaxpr/qhc,khc->hqk/dot_general | solution.py:80
  476.6 12.7 %multiply_convert_fusion = bf16[12,576,576]{1,2,0:T(8,128)(2,1)S(1)} fusion(f32[12,576,576]{1,2,0:T(8,128)} %get-tuple-element.93, f32[12,576,576]{1,2,0:T(8,128)} %get-tuple-element.84, f32[12,576]{1,0:T(8,128)S(1)} %get-tuple-element.92, f32[12,576]{1,0:T(8,128)S(1)} %copy-done.22), kind=kLoop, calls=%fused_computation.2 | loop fusion | flops 15925248 | bytes 39868416 | tf_op jit(solution)/shard_map/while/body/eval_jaxpr/convert_element_type | solution.py:86
  489.3 2.7 multiply_convert_fusion.1
  492.0 1.7 multiply_convert_fusion.2
  493.8 9.2 %fusion.82 = bf16[12,64,576]{2,1,0:T(8,128)(2,1)S(1)} fusion(bf16[576,12,64]{0,2,1:T(8,128)(2,1)S(1)} %bitcast.98, f32[12,576,576]{1,2,0:T(8,128)} %get-tuple-element.84, f32[12,576]{1,0:T(8,128)S(1)} %copy-done.22), kind=kOutput, calls=%fused_computation.122 | convolution fusion | flops 518012928 | bytes 17722368 | tf_op jit(solution)/shard_map/while/body/eval_jaxpr/hqk,qhc->khc/dot_general | solution.py:81
  503.1 0.9 copy-done.18
  504.0 6.3 fusion.88
  510.4 1.1 copy-done.6
  511.5 0.8 fusion.145
  512.3 1.8 reduce_sum.267
  514.9 11.2 %all-reduce.11 = (bf16[1,3072]{1,0:T(2,128)(2,1)S(1)}, bf16[1,768]{1,0:T(2,128)(2,1)S(1)}) all-reduce(bf16[1,3072]{1,0:T(2,128)(2,1)S(1)} %broadcast_in_dim.62, bf16[1,768]{1,0:T(2,128)(2,1)S(1)} %broadcast_in_dim.66), channel_id=1, replica_groups=mesh['exp'=8,'rep'=4] {'rep'}, use_global_device_ids=true, to_apply=%region_36.37 | all-reduce | flops 3840 | bytes 15360 | tf_op jit(solution)/shard_map/psum | solution.py:232
  527.3 6.9 fusion.64
  534.3 39.1 %all-reduce.9 = (f32[768]{0:T(1024)S(1)}, f32[768]{0:T(1024)S(1)}, f32[768]{0:T(1024)S(1)}, f32[768]{0:T(1024)S(1)}, f32[768,8]{0,1:T(8,128)S(1)}) all-reduce(f32[768]{0:T(1024)S(1)} %get-tuple-element.50, f32[768]{0:T(1024)S(1)} %get-tuple-element.55, f32[768]{0:T(1024)S(1)} %copy-done.32, ...), channel_id=2, replica_groups=mesh['exp'=8,'rep'=4] {'exp','rep'}, use_global_device_ids=true, to_apply=%region_24.25.clone | all-reduce | flops 9216 | bytes 73728
  576.4 3.3 fusion.63
  579.7 19.2 %all-reduce.15.cloned.1.call-done = (bf16[1,768,3072]{2,1,0:T(8,128)(2,1)}, bf16[1,3072,768]{2,1,0:T(8,128)(2,1)}) async-done(((bf16[1,768,3072]{2,1,0:T(8,128)(2,1)}, bf16[1,3072,768]{2,1,0:T(8,128)(2,1)}), (bf16[1,768,3072]{2,1,0:T(8,128)(2,1)}, bf16[1,3072,768]{2,1,0:T(8,128)(2,1)})) %all-reduce.15.cloned.1.call-update) | async-done | bytes 9437200 | tf_op jit(solution)/shard_map/psum | solution.py:231
  598.8 7.5 broadcast_in_dim.61
  606.4 4.5 broadcast_in_dim.65
  610.8 93.4 %reduce-scatter.6.cloned.1.call-done = f32[24,768]{1,0:T(8,128)} async-done(((f32[768,768]{1,0:T(8,128)}), f32[24,768]{1,0:T(8,128)}) %reduce-scatter.6.cloned.1.call-update) | async-done | bytes 73744 | tf_op jit(solution)/shard_map/reduce_scatter | solution.py:296
  704.2 124.8 %reduce-scatter.4.cloned.1.call-done = f32[24,2304]{1,0:T(8,128)} async-done(((f32[768,2304]{1,0:T(8,128)}), f32[24,2304]{1,0:T(8,128)}) %reduce-scatter.4.cloned.1.call-update) | async-done | bytes 221200 | tf_op jit(solution)/shard_map/reduce_scatter | solution.py:295
  (162 shorter events, 15.7 us)
Async XLA Ops:
  7.2 66.5 %all-gather.4.cloned.1.call-start = ((), (), s32[]{:S(2)}) async-start(), calls=%async_computation.6 | async-start | bytes 3649536 | tf_op jit(solution)/shard_map/all_gather | solution.py:152
  7.9 121.5 %all-gather.6.cloned.1.call-start = ((), (), s32[]{:S(2)}) async-start(), calls=%async_computation.7 | async-start | bytes 1216512 | tf_op jit(solution)/shard_map/all_gather | solution.py:153
  57.7 20.7 %copy-start.41 = (f32[768]{0:T(1024)}, f32[768]{0:T(1024)S(1)}, u32[]{:S(2)}) copy-start(f32[768]{0:T(1024)S(1)} %convert_element_type.191) | copy-start | bytes 9220
  58.6 19.8 %copy-start.34 = (f32[768]{0:T(1024)}, f32[768]{0:T(1024)S(1)}, u32[]{:S(2)}) copy-start(f32[768]{0:T(1024)S(1)} %convert_element_type.190) | copy-start | bytes 9220
  58.6 392.7 %copy-start.24 = (f32[768]{0:T(1024)}, f32[768]{0:T(1024)S(1)}, u32[]{:S(2)}) copy-start(f32[768]{0:T(1024)S(1)} %convert_element_type.199) | copy-start | bytes 9220
  60.0 18.4 %copy-start.26 = (f32[576]{0:T(1024)}, f32[576]{0:T(1024)S(1)}, u32[]{:S(2)}) copy-start(f32[576]{0:T(1024)S(1)} %broadcast_multiply_fusion.5) | copy-start | bytes 6916
  61.6 16.8 %copy-start.37 = (f32[576]{0:T(1024)}, f32[576]{0:T(1024)S(1)}, u32[]{:S(2)}) copy-start(f32[576]{0:T(1024)S(1)} %add_rsqrt_fusion.1) | copy-start | bytes 6916
  80.1 11.2 %copy-start.1 = (bf16[576,768]{0,1:T(8,128)(2,1)}, bf16[576,768]{0,1:T(8,128)(2,1)S(1)}, u32[]{:S(2)}) copy-start(bf16[576,768]{0,1:T(8,128)(2,1)S(1)} %copy.62) | copy-start | bytes 2654212
  82.0 9.4 %copy-start.3 = (bf16[576,768]{0,1:T(8,128)(2,1)}, bf16[576,768]{0,1:T(8,128)(2,1)S(1)}, u32[]{:S(2)}) copy-start(bf16[576,768]{0,1:T(8,128)(2,1)S(1)} %copy.61) | copy-start | bytes 2654212
  91.4 8.6 %copy-start.13 = (bf16[576,768]{0,1:T(8,128)(2,1)S(1)}, bf16[576,768]{0,1:T(8,128)(2,1)}, u32[]{:S(2)}) copy-start(bf16[576,768]{0,1:T(8,128)(2,1)} %copy.60) | copy-start | bytes 2654212
  100.0 29.4 %copy-start.7 = (bf16[576,768]{1,0:T(8,128)(2,1)S(1)}, bf16[576,768]{1,0:T(8,128)(2,1)}, u32[]{:S(2)}) copy-start(bf16[576,768]{1,0:T(8,128)(2,1)} %param.17) | copy-start | bytes 2654212
  132.3 319.0 %copy-start.25 = (f32[576]{0:T(1024)}, f32[576]{0:T(1024)S(1)}, u32[]{:S(2)}) copy-start(f32[576]{0:T(1024)S(1)} %add_rsqrt_fusion) | copy-start | bytes 6916
  132.6 181.8 %copy-start.5 = (bf16[576,768]{1,0:T(8,128)(2,1)}, bf16[576,768]{1,0:T(8,128)(2,1)S(1)}, u32[]{:S(2)}) copy-start(bf16[576,768]{1,0:T(8,128)(2,1)S(1)} %add_convert_fusion.2) | copy-start | bytes 2654212
  136.2 5.1 copy-start.40
  136.2 5.2 copy-start.43
  136.2 49.0 %all-to-all-start = ((bf16[8,152,768]{2,1,0:T(8,128)(2,1)}), bf16[8,152,768]{2,1,0:T(8,128)(2,1)}, u32[]{:S(2)}, u32[]{:S(2)}) async-start(bf16[8,152,768]{2,1,0:T(8,128)(2,1)} %bitcast.105), calls=%async_computation | async-start | bytes 3735552 | tf_op jit(solution)/shard_map/all_to_all | solution.py:181
  197.9 34.2 %copy-start = (f32[8,152,3072]{2,1,0:T(8,128)}, f32[8,152,3072]{2,1,0:T(8,128)S(1)}, u32[]{:S(2)}) copy-start(f32[8,152,3072]{2,1,0:T(8,128)S(1)} %get-tuple-element.87) | copy-start | bytes 44826628
  232.0 3.1 copy-start.10
  244.5 4.5 copy-start.44
  244.5 70.3 %all-to-all-start.1 = ((bf16[8,152,768]{2,1,0:T(8,128)(2,1)}), bf16[8,152,768]{2,1,0:T(8,128)(2,1)}, u32[]{:S(2)}, u32[]{:S(2)}) async-start(bf16[8,152,768]{2,1,0:T(8,128)(2,1)} %add_convert_fusion), calls=%async_computation.1 | async-start | bytes 3735552 | tf_op jit(solution)/shard_map/all_to_all | solution.py:189
  314.9 3.1 copy-start.20
  318.0 5.0 copy-start.15
  318.0 59.8 %slice-start = ((s8[14942208]{0:T(1024)(128)(4,1)}), s8[4194304]{0:T(1024)(128)(4,1)S(1)}, s32[]{:S(2)}) async-start(s8[14942208]{0:T(1024)(128)(4,1)} %bitcast.93), calls=%async_computation.11 | async-start | bytes 8388608
  318.0 59.8 %slice-start.1 = ((s8[14942208]{0:T(1024)(128)(4,1)}), s8[4194304]{0:T(1024)(128)(4,1)S(1)}, s32[]{:S(2)}) async-start(s8[14942208]{0:T(1024)(128)(4,1)} %bitcast.93), calls=%async_computation.12 | async-start | bytes 8388608
  323.0 2.2 copy-start.28
  323.0 2.2 copy-start.30
  323.1 54.7 %slice-start.2 = ((s8[14942208]{0:T(1024)(128)(4,1)}), s8[4194304]{0:T(1024)(128)(4,1)S(1)}, s32[]{:S(2)}) async-start(s8[14942208]{0:T(1024)(128)(4,1)} %bitcast.93), calls=%async_computation.13 | async-start | bytes 8388608
  323.1 54.7 %slice-start.4 = ((s8[4718592]{0:T(1024)(128)(4,1)}), s8[4194304]{0:T(1024)(128)(4,1)S(1)}, s32[]{:S(2)}) async-start(s8[4718592]{0:T(1024)(128)(4,1)} %bitcast.118), calls=%async_computation.15 | async-start | bytes 8388608
  325.2 52.6 %slice-start.3 = ((s8[14942208]{0:T(1024)(128)(4,1)}), s8[2359296]{0:T(1024)(128)(4,1)S(1)}, s32[]{:S(2)}) async-start(s8[14942208]{0:T(1024)(128)(4,1)} %bitcast.93), calls=%async_computation.14 | async-start | bytes 4718592
  325.2 52.6 %slice-start.5 = ((s8[4718592]{0:T(1024)(128)(4,1)}), s8[524288]{0:T(1024)(128)(4,1)S(1)}, s32[]{:S(2)}) async-start(s8[4718592]{0:T(1024)(128)(4,1)} %bitcast.118), calls=%async_computation.16 | async-start | bytes 1048576
  377.8 12.3 %copy-start.11 = (bf16[8,152,768]{2,1,0:T(8,128)(2,1)}, bf16[8,152,768]{2,1,0:T(8,128)(2,1)S(1)}, u32[]{:S(2)}) copy-start(bf16[8,152,768]{2,1,0:T(8,128)(2,1)S(1)} %all_to_all.20) | copy-start | bytes 5603332
  400.9 46.9 %all-to-all-start.3 = ((bf16[8,152,768]{2,1,0:T(8,128)(2,1)}), bf16[8,152,768]{2,1,0:T(8,128)(2,1)}, u32[]{:S(2)}, u32[]{:S(2)}) async-start(bf16[8,152,768]{2,1,0:T(8,128)(2,1)} %fusion.55), calls=%async_computation.3 | async-start | bytes 3735552 | tf_op jit(solution)/shard_map/all_to_all | solution.py:239
  405.2 193.6 %all-reduce.15.cloned.1.call-start = ((), (), s32[]{:S(2)}) async-start(), calls=%async_computation.10 | async-start | bytes 18874368 | tf_op jit(solution)/shard_map/psum | solution.py:231
  426.8 277.5 %reduce-scatter.6.cloned.1.call-start = ((), (), s32[]{:S(2)}) async-start(), calls=%async_computation.9 | async-start | bytes 2433024 | tf_op jit(solution)/shard_map/reduce_scatter | solution.py:296
  451.3 1.7 copy-start.16
  451.3 2.1 copy-start.17
  451.3 2.3 copy-start.21
  451.4 2.3 copy-start.29
  451.4 2.3 copy-start.31
  453.7 2.8 copy-start.45
  459.8 4.2 copy-start.22
  463.6 365.4 %reduce-scatter.4.cloned.1.call-start = ((), (), s32[]{:S(2)}) async-start(), calls=%async_computation.8 | async-start | bytes 7299072 | tf_op jit(solution)/shard_map/reduce_scatter | solution.py:295
  476.6 12.7 %copy-start.4 = (bf16[576,768]{0,1:T(8,128)(2,1)S(1)}, bf16[576,768]{0,1:T(8,128)(2,1)}, u32[]{:S(2)}) copy-start(bf16[576,768]{0,1:T(8,128)(2,1)} %copy-done.3) | copy-start | bytes 2654212
  489.3 2.7 copy-start.2
  492.0 11.0 %copy-start.19 = (bf16[12,64,576]{2,1,0:T(8,128)(2,1)}, bf16[12,64,576]{2,1,0:T(8,128)(2,1)S(1)}, u32[]{:S(2)}) copy-start(bf16[12,64,576]{2,1,0:T(8,128)(2,1)S(1)} %multiply_convert_fusion.1) | copy-start | bytes 2654212
  493.7 9.3 %copy-start.14 = (bf16[12,64,576]{2,1,0:T(8,128)(2,1)}, bf16[12,64,576]{2,1,0:T(8,128)(2,1)S(1)}, u32[]{:S(2)}) copy-start(bf16[12,64,576]{2,1,0:T(8,128)(2,1)S(1)} %multiply_convert_fusion.2) | copy-start | bytes 2654212
  493.7 10.3 %copy-start.8 = (bf16[576,768]{1,0:T(8,128)(2,1)S(1)}, bf16[576,768]{1,0:T(8,128)(2,1)}, u32[]{:S(2)}) copy-start(bf16[576,768]{1,0:T(8,128)(2,1)} %param.17) | copy-start | bytes 2654212
  493.7 10.2 %copy-start.27 = (f32[576]{0:T(1024)S(1)}, f32[576]{0:T(1024)}, u32[]{:S(2)}) copy-start(f32[576]{0:T(1024)} %copy-done.26) | copy-start | bytes 6916
  493.8 10.2 %copy-start.35 = (f32[768]{0:T(1024)S(1)}, f32[768]{0:T(1024)}, u32[]{:S(2)}) copy-start(f32[768]{0:T(1024)} %copy-done.34) | copy-start | bytes 9220
  493.8 10.2 %copy-start.38 = (f32[576]{0:T(1024)S(1)}, f32[576]{0:T(1024)}, u32[]{:S(2)}) copy-start(f32[576]{0:T(1024)} %copy-done.37) | copy-start | bytes 6916
  493.8 10.2 %copy-start.42 = (f32[768]{0:T(1024)S(1)}, f32[768]{0:T(1024)}, u32[]{:S(2)}) copy-start(f32[768]{0:T(1024)} %copy-done.41) | copy-start | bytes 9220
  503.0 0.9 copy-start.18
  510.3 1.2 copy-start.6
  510.3 17.0 %copy-start.9 = (bf16[576,768]{1,0:T(8,128)(2,1)S(1)}, bf16[576,768]{1,0:T(8,128)(2,1)}, u32[]{:S(2)}) copy-start(bf16[576,768]{1,0:T(8,128)(2,1)} %param.17) | copy-start | bytes 2654212
  527.3 7.0 copy-start.23
  527.3 7.0 copy-start.32
  527.3 7.0 copy-start.33
  527.3 49.1 %copy-start.36 = (f32[768]{0:T(1024)S(1)}, f32[768]{0:T(1024)}, u32[]{:S(2)}) copy-start(f32[768]{0:T(1024)} %copy-done.34) | copy-start | bytes 9220
  527.3 49.1 %copy-start.39 = (f32[576]{0:T(1024)S(1)}, f32[576]{0:T(1024)}, u32[]{:S(2)}) copy-start(f32[576]{0:T(1024)} %copy-done.37) | copy-start | bytes 6916
  598.8 7.5 copy-start.12
Sparse Core Ops, SparseCore 0:
  10.9 62.7 all-gather.3
  76.6 52.7 all-gather.5
  426.9 171.9 all-reduce.14
  604.6 99.6 reduce-scatter.5
  710.3 118.6 reduce-scatter.3
where the time goes:
time: 843 us; the launch traced here: 836 us
  waiting for transfers between devices  331 us (39%)
  blocking collectives  208 us (25%)
  matrix products  162 us (19%)
  other arithmetic  85.2 us (10%)
  local copies, waits for them, and re-layouts  20.4 us (2%)
  between operations  14.8 us (2%)
  starting transfers between devices  14.7 us (2%)
    reduce_scatter x1, waiting for transfers between devices, on_device(): lax.psum_scatter(grad_qkv_weight, ('exp', 'rep'), scatter_dimension=0, ti...  125 us
    reduce_scatter x1, waiting for transfers between devices, on_device(): lax.psum_scatter(grad_out_weight, ('exp', 'rep'), scatter_dimension=0, ti...  93.4 us
    unnamed x2, blocking collectives  81.3 us
    all_gather x1, blocking collectives, on_device(): lax.all_gather(w_router, ('exp', 'rep'), axis=0, tiled=True)  65.3 us
    all_to_all x1, blocking collectives, on_device(): lax.all_to_all(grad_slots.astype(jnp.bfloat16).reshape(experts, capacity,...  50.3 us
    all_to_all x1, waiting for transfers between devices, on_device(): lax.all_to_all(buffer, 'exp', split_axis=0, concat_axis=0, tiled=True)  43.8 us
    convert_element_type x1, other arithmetic, on_device(): active_part = jax.nn.gelu(pre_part, approximate=False).astype(jnp.bfloat16)  34.1 us
    all_to_all x1, waiting for transfers between devices, on_device(): lax.all_to_all(grad_received, 'exp', split_axis=0, concat_axis=0, tiled=T...  20.3 us
  transfers between devices with their start and end apart: 8, of which 7 were waited for; matrix products, arithmetic and copies ran while one was open for 19% of the time, Pallas kernels for 0%

commit v1 on v0

--- a/solution.py
+++ b/solution.py
@@ -228,7 +228,9 @@
     )
     grad_b_in = jnp.sum(grad_pre.astype(jnp.float32), axis=(0, 1))
     expert_sums = (
-        lax.psum(grad_w_in.astype(jnp.bfloat16), "rep").astype(jnp.float32),
+        jnp.sum(lax.all_gather(grad_w_in.astype(jnp.bfloat16), axis_name="rep"), axis=0).astype(
+            jnp.float32
+        ),
         lax.psum(grad_b_in.astype(jnp.bfloat16), "rep").astype(jnp.float32),
         lax.psum(grad_w_back.astype(jnp.bfloat16), "rep").astype(jnp.float32),
         lax.psum(grad_b_back.astype(jnp.bfloat16), "rep").astype(jnp.float32),

time: 843 us -> 847 us (level)
  waiting for transfers between devices: 331 us -> 314 us
  other arithmetic: 85.2 us -> 101 us
    all_to_all x1, waiting for transfers between devices: 20.3 us -> 41.5 us  [on_device(): lax.all_to_all(grad_received, 'exp', split_axis=0, concat_axis=0, tiled=T...]
    psum x1, waiting for transfers between devices: 19.2 us -> 0.01 us  [on_device(): lax.psum(grad_w_back.astype(jnp.bfloat16), 'rep').astype(jnp.float32)]
    reduce_scatter x1, waiting for transfers between devices: 93.4 us -> 74.4 us  [on_device(): lax.psum_scatter(grad_out_weight, ('exp', 'rep'), scatter_dimension=0, ti...]
    reduce_sum x0 -> x1, other arithmetic: none -> 14 us  [on_device(): jnp.sum(lax.all_gather(grad_w_in.astype(jnp.bfloat16), axis_name='rep'),...]
  transfers between devices with their start and end apart: 8 -> 9, of which waited for: 7 -> 6; matrix products, arithmetic and copies ran while one was open for 19% -> 23% of each run, Pallas kernels for 0% -> 0%
where the time goes in v1:
time: 847 us; the launch traced here: 840 us
  waiting for transfers between devices  314 us (37%)
  blocking collectives  209 us (25%)
  matrix products  161 us (19%)
  other arithmetic  101 us (12%)
  local copies, waits for them, and re-layouts  24 us (3%)
  between operations  15.1 us (2%)
  starting transfers between devices  14.8 us (2%)
    reduce_scatter x1, waiting for transfers between devices, on_device(): lax.psum_scatter(grad_qkv_weight, ('exp', 'rep'), scatter_dimension=0, ti...  125 us
    unnamed x2, blocking collectives  81.8 us
    reduce_scatter x1, waiting for transfers between devices, on_device(): lax.psum_scatter(grad_out_weight, ('exp', 'rep'), scatter_dimension=0, ti...  74.4 us
    all_gather x1, blocking collectives, on_device(): lax.all_gather(w_router, ('exp', 'rep'), axis=0, tiled=True)  65.3 us
    all_to_all x1, blocking collectives, on_device(): lax.all_to_all(grad_slots.astype(jnp.bfloat16).reshape(experts, capacity,...  50.3 us
    all_to_all x1, waiting for transfers between devices, on_device(): lax.all_to_all(buffer, 'exp', split_axis=0, concat_axis=0, tiled=True)  43.8 us
    all_to_all x1, waiting for transfers between devices, on_device(): lax.all_to_all(grad_received, 'exp', split_axis=0, concat_axis=0, tiled=T...  41.5 us
    convert_element_type x1, other arithmetic, on_device(): active_part = jax.nn.gelu(pre_part, approximate=False).astype(jnp.bfloat16)  34.1 us
  transfers between devices with their start and end apart: 9, of which 6 were waited for; matrix products, arithmetic and copies ran while one was open for 23% of the time, Pallas kernels for 0%

profile of v1, /device:TPU:0, one launch (start us, length us, event | category | flops | bytes accessed | tf_op | source)
XLA Modules:
  0.0 839.5 jit_solution(6037891693056788416)
XLA Ops:
  10.2 1.2 fusion.101
  12.1 0.8 dynamic-update-slice.3
  13.0 0.8 dynamic-update-slice
  14.6 0.8 dynamic-update-slice.2
  15.5 42.2 %all-reduce.10 = (bf16[768]{0:T(1024)(128)(2,1)S(1)}, bf16[768]{0:T(1024)(128)(2,1)S(1)}, bf16[768]{0:T(1024)(128)(2,1)S(1)}, bf16[768]{0:T(1024)(128)(2,1)S(1)}) all-reduce(bf16[768]{0:T(1024)(128)(2,1)S(1)} %dynamic-update-slice.1, bf16[768]{0:T(1024)(128)(2,1)S(1)} %dynamic-update-slice, ...), channel_id=1, replica_groups=mesh['exp'=8,'rep'=4] {'exp','rep'}, use_global_device_ids=true, to_apply=%add.1 | all-reduce | flops 3072 | bytes 12288
  58.6 1.4 convert_reduce_fusion
  60.0 1.6 fusion.64
  62.4 1.2 fusion.98
  64.7 9.0 %all-gather.6.cloned.1.call-done = bf16[768,2304]{1,0:T(8,128)(2,1)} async-done(((bf16[24,2304]{1,0:T(8,128)(2,1)}), bf16[768,2304]{1,0:T(8,128)(2,1)}) %all-gather.6.cloned.1.call-update) | async-done | bytes 3538960 | tf_op jit(solution)/shard_map/all_gather | solution.py:152
  73.7 4.7 convolution_convert_fusion
  78.4 1.1 fusion.139
  80.1 1.9 copy.61
  82.0 1.3 copy.60
  83.3 8.0 fusion.140
  91.4 8.6 %fusion = f32[12,576]{1,0:T(8,128)S(1)} fusion(f32[12,576,576]{1,2,0:T(8,128)} %get-tuple-element.82, f32[12,576]{1,0:T(8,128)S(1)} %get-tuple-element.81), kind=kLoop, calls=%fused_computation.8 | loop fusion | flops 7955712 | bytes 15980544 | tf_op jit(solution)/shard_map/while/body/eval_jaxpr/reduce_sum | solution.py:70
  100.0 10.4 %fusion.80 = bf16[12,64,576]{2,1,0:T(8,128)(2,1)} fusion(bf16[576,12,64]{0,2,1:T(8,128)(2,1)S(1)} %bitcast.103, f32[12,576,576]{1,2,0:T(8,128)} %get-tuple-element.82, f32[12,576]{1,0:T(8,128)S(1)} %fusion, f32[12,576]{1,0:T(8,128)S(1)} %get-tuple-element.81), kind=kOutput, calls=%fused_computation.121 | convolution fusion | flops 521994240 | bytes 17750016 | tf_op jit(solution)/shard_map/while/body/eval_jaxpr/hqk,khc->qhc/dot_general | solution.py:72
  110.4 18.9 %all-gather.8.cloned.1.call-done = bf16[768,768]{1,0:T(8,128)(2,1)} async-done(((bf16[24,768]{1,0:T(8,128)(2,1)}), bf16[768,768]{1,0:T(8,128)(2,1)}) %all-gather.8.cloned.1.call-update) | async-done | bytes 1179664 | tf_op jit(solution)/shard_map/all_gather | solution.py:153
  129.4 2.6 fusion.141
  132.7 3.5 convolution_convert_fusion.1
  136.2 5.1 all-to-all-start
  141.4 43.8 %all-to-all-done = bf16[8,152,768]{2,1,0:T(8,128)(2,1)} async-done(((bf16[8,152,768]{2,1,0:T(8,128)(2,1)}), bf16[8,152,768]{2,1,0:T(8,128)(2,1)}, u32[]{:S(2)}, u32[]{:S(2)}) %all-to-all-start) | async-done | bytes 1867808 | tf_op jit(solution)/shard_map/all_to_all | solution.py:181
  185.2 12.7 %fusion.29 = (u8[152,3072]{1,0:T(8,128)(4,1)S(1)}, u8[152,3072]{1,0:T(8,128)(4,1)S(1)}, f32[8,152,3072]{2,1,0:T(8,128)S(1)}) fusion(f32[3072]{0:T(1024)S(1)} %bitcast.114, bf16[8,152,768]{2,1,0:T(8,128)(2,1)} %all-to-all-done, bf16[1,768,3072]{2,1,0:T(8,128)(2,1)} %param.25), kind=kOutput, calls=%fused_computation.54 | convolution fusion | flops 5789171712 | bytes 22474752 | tf_op jit(solution)/shard_map/scd,df->scf/dot_general | solution.py:182
  197.9 34.1 %fusion.3 = bf16[8,152,3072]{2,1,0:T(8,128)(2,1)S(1)} fusion(f32[8,152,3072]{2,1,0:T(8,128)S(1)} %get-tuple-element.85, f32[3072]{0:T(1024)S(1)} %bitcast.115, u8[152,3072]{1,0:T(8,128)(4,1)S(1)} %get-tuple-element.47, u8[152,3072]{1,0:T(8,128)(4,1)S(1)} %get-tuple-element.46), kind=kLoop, calls=%fused_computation.11 | loop fusion | flops 265224192 | bytes 23359488 | tf_op jit(solution)/shard_map/convert_element_type | solution.py:185
  232.1 3.1 copy-done.10
  235.1 9.4 %add_convert_fusion = bf16[8,152,768]{2,1,0:T(8,128)(2,1)} fusion(f32[768]{0:T(1024)S(1)} %convert_reduce_fusion.2, bf16[8,152,3072]{2,1,0:T(8,128)(2,1)S(1)} %fusion.3, bf16[1,3072,768]{2,1,0:T(8,128)(2,1)} %param.27), kind=kOutput, calls=%fused_computation.52 | convolution fusion | flops 5739675648 | bytes 14060544 | tf_op jit(solution)/shard_map/scf,fd->scd/dot_general | solution.py:186
  244.6 4.5 all-to-all-start.1
  249.1 65.3 %all-gather.1 = bf16[32,24,8]{1,2,0:T(8,128)(2,1)S(1)} all-gather(bf16[1,24,8]{1,2,0:T(8,128)(2,1)S(1)} %bitcast.117), channel_id=1, replica_groups=mesh['exp'=8,'rep'=4] {'exp','rep'}, dimensions={0}, use_global_device_ids=true | all-gather | bytes 12672 | tf_op jit(solution)/shard_map/all_gather | solution.py:156
  314.9 3.1 fusion.39
  318.1 5.0 fusion.67
  323.2 2.1 fusion.32
  325.3 2.3 fusion.30
  327.6 50.3 %all_to_all.20 = bf16[8,152,768]{2,1,0:T(8,128)(2,1)S(1)} all-to-all(bf16[8,152,768]{2,1,0:T(8,128)(2,1)S(1)} %bitcast.107), channel_id=1, replica_groups=mesh['exp'=8,'rep'=4] {'exp'}, dimensions={0} | all-to-all | bytes 3735552 | tf_op jit(solution)/shard_map/all_to_all | solution.py:207
  377.9 1.3 copy-done.11
  379.2 8.2 fusion.27
  387.7 15.0 %fusion.143 = (bf16[3072]{0:T(1024)(128)(2,1)}, bf16[8,152,3072]{2,1,0:T(8,128)(2,1)S(1)}) fusion(f32[8,152,3072]{2,1,0:T(8,128)} %copy-done, f32[3072]{0:T(1024)S(1)} %bitcast.116, bf16[8,152,768]{2,1,0:T(8,128)(2,1)} %copy-done.11, bf16[1,3072,768]{2,1,0:T(8,128)(2,1)} %param.27), kind=kOutput, calls=%fused_computation.194 | convolution fusion | flops 5782631424 | bytes 29018112 | tf_op jit(solution)/shard_map/scd,fd->scf/dot_general | solution.py:222
  402.6 3.1 copy-done.47
  405.7 9.4 %bitcast_convert_fusion.1 = bf16[768,3072]{1,0:T(8,128)(2,1)} fusion(bf16[8,152,768]{2,1,0:T(8,128)(2,1)} %all-to-all-done, bf16[8,152,3072]{2,1,0:T(8,128)(2,1)S(1)} %get-tuple-element.94), kind=kOutput, calls=%fused_computation.37 | convolution fusion | flops 5740167168 | bytes 14057472 | tf_op jit(solution)/shard_map/scd,scf->df/dot_general | solution.py:226
  415.1 10.8 %fusion.54 = bf16[8,152,768]{2,1,0:T(8,128)(2,1)} fusion(bf16[8,152,3072]{2,1,0:T(8,128)(2,1)} %copy-done.47, bf16[1,768,3072]{2,1,0:T(8,128)(2,1)} %param.25), kind=kOutput, calls=%fused_computation.87 | convolution fusion | flops 5738741760 | bytes 14057472 | tf_op jit(solution)/shard_map/scf,df->scd/dot_general | solution.py:238
  425.9 4.3 all-to-all-start.3
  430.9 41.5 %all-to-all-done.3 = bf16[8,152,768]{2,1,0:T(8,128)(2,1)} async-done(((bf16[8,152,768]{2,1,0:T(8,128)(2,1)}), bf16[8,152,768]{2,1,0:T(8,128)(2,1)}, u32[]{:S(2)}, u32[]{:S(2)}) %all-to-all-start.3) | async-done | bytes 1867808 | tf_op jit(solution)/shard_map/all_to_all | solution.py:241
  472.5 3.6 fusion.84
  476.1 1.6 multiply_reduce_fusion.1
  478.3 2.8 convert_add_fusion
  481.1 1.8 convolution_convert_fusion.2
  482.9 1.5 copy.65
  484.4 3.7 fusion.112
  488.6 16.1 %multiply_reduce_fusion = (f32[12,576]{1,0:T(8,128)S(1)}, f32[12,576,576]{1,2,0:T(8,128)}) fusion(f32[12,576,576]{1,2,0:T(8,128)} %get-tuple-element.82, f32[12,576]{1,0:T(8,128)S(1)} %copy-done.24, bf16[576,12,64]{0,2,1:T(8,128)(2,1)S(1)} %bitcast.96, bf16[576,12,64]{0,2,1:T(8,128)(2,1)} %bitcast.102), kind=kOutput, calls=%fused_computation.3 | convolution fusion | flops 521544960 | bytes 33675264 | tf_op jit(solution)/shard_map/while/body/eval_jaxpr/qhc,khc->hqk/dot_general | solution.py:80
  504.8 12.5 %multiply_convert_fusion = bf16[12,576,576]{1,2,0:T(8,128)(2,1)S(1)} fusion(f32[12,576,576]{1,2,0:T(8,128)} %get-tuple-element.91, f32[12,576,576]{1,2,0:T(8,128)} %get-tuple-element.82, f32[12,576]{1,0:T(8,128)S(1)} %get-tuple-element.90, f32[12,576]{1,0:T(8,128)S(1)} %copy-done.24), kind=kLoop, calls=%fused_computation.2 | loop fusion | flops 15925248 | bytes 39868416 | tf_op jit(solution)/shard_map/while/body/eval_jaxpr/convert_element_type | solution.py:86
  517.3 2.7 multiply_convert_fusion.1
  520.0 1.7 multiply_convert_fusion.2
  521.7 9.3 %fusion.81 = bf16[12,64,576]{2,1,0:T(8,128)(2,1)S(1)} fusion(bf16[576,12,64]{0,2,1:T(8,128)(2,1)S(1)} %bitcast.97, f32[12,576,576]{1,2,0:T(8,128)} %get-tuple-element.82, f32[12,576]{1,0:T(8,128)S(1)} %copy-done.24), kind=kOutput, calls=%fused_computation.122 | convolution fusion | flops 518012928 | bytes 17722368 | tf_op jit(solution)/shard_map/while/body/eval_jaxpr/hqk,qhc->khc/dot_general | solution.py:81
  531.1 0.9 copy-done.18
  532.0 6.2 fusion.87
  538.3 1.1 copy-done.6
  539.7 1.9 reduce_sum.280
  541.6 12.0 %all-reduce.11 = (bf16[1,3072]{1,0:T(2,128)(2,1)S(1)}, bf16[1,768]{1,0:T(2,128)(2,1)S(1)}) all-reduce(bf16[1,3072]{1,0:T(2,128)(2,1)S(1)} %broadcast_in_dim.55, bf16[1,768]{1,0:T(2,128)(2,1)S(1)} %broadcast_in_dim.59), channel_id=1, replica_groups=mesh['exp'=8,'rep'=4] {'rep'}, use_global_device_ids=true, to_apply=%region_36.37 | all-reduce | flops 3840 | bytes 15360 | tf_op jit(solution)/shard_map/psum | solution.py:234
  554.8 7.0 broadcast_in_dim.58
  561.8 4.1 fusion.63
  565.9 39.6 %all-reduce.9 = (f32[768]{0:T(1024)S(1)}, f32[768]{0:T(1024)S(1)}, f32[768]{0:T(1024)S(1)}, f32[768]{0:T(1024)S(1)}, f32[768,8]{0,1:T(8,128)S(1)}) all-reduce(f32[768]{0:T(1024)S(1)} %get-tuple-element.50, f32[768]{0:T(1024)S(1)} %get-tuple-element.55, f32[768]{0:T(1024)S(1)} %copy-done.33, ...), channel_id=3, replica_groups=mesh['exp'=8,'rep'=4] {'exp','rep'}, use_global_device_ids=true, to_apply=%region_24.25.clone | all-reduce | flops 9216 | bytes 73728
  608.6 3.3 fusion.62
  611.9 14.0 %reduce_sum.278 = bf16[768,3072]{1,0:T(8,128)(2,1)} reduce(bf16[4,768,3072]{2,1,0:T(8,128)(2,1)} %bitcast.93, bf16[]{:T(256)} %constant.50.clone.1), dimensions={0}, to_apply=%region_34.35 | reduce | flops 7077888 | bytes 23592962 | tf_op jit(solution)/shard_map/reduce_sum | solution.py:231
  625.9 7.4 bitcast_convert_fusion.2
  633.3 74.4 %reduce-scatter.6.cloned.1.call-done = f32[24,768]{1,0:T(8,128)} async-done(((f32[768,768]{1,0:T(8,128)}), f32[24,768]{1,0:T(8,128)}) %reduce-scatter.6.cloned.1.call-update) | async-done | bytes 73744 | tf_op jit(solution)/shard_map/reduce_scatter | solution.py:298
  707.7 124.7 %reduce-scatter.4.cloned.1.call-done = f32[24,2304]{1,0:T(8,128)} async-done(((f32[768,2304]{1,0:T(8,128)}), f32[24,2304]{1,0:T(8,128)}) %reduce-scatter.4.cloned.1.call-update) | async-done | bytes 221200 | tf_op jit(solution)/shard_map/reduce_scatter | solution.py:297
  (161 shorter events, 15.9 us)
Async XLA Ops:
  7.2 66.5 %all-gather.6.cloned.1.call-start = ((), (), s32[]{:S(2)}) async-start(), calls=%async_computation.6 | async-start | bytes 3649536 | tf_op jit(solution)/shard_map/all_gather | solution.py:152
  7.9 121.5 %all-gather.8.cloned.1.call-start = ((), (), s32[]{:S(2)}) async-start(), calls=%async_computation.7 | async-start | bytes 1216512 | tf_op jit(solution)/shard_map/all_gather | solution.py:153
  57.7 20.7 %copy-start.41 = (f32[768]{0:T(1024)}, f32[768]{0:T(1024)S(1)}, u32[]{:S(2)}) copy-start(f32[768]{0:T(1024)S(1)} %convert_element_type.205) | copy-start | bytes 9220
  58.6 19.8 %copy-start.35 = (f32[768]{0:T(1024)}, f32[768]{0:T(1024)S(1)}, u32[]{:S(2)}) copy-start(f32[768]{0:T(1024)S(1)} %convert_element_type.204) | copy-start | bytes 9220
  58.6 417.4 %copy-start.25 = (f32[768]{0:T(1024)}, f32[768]{0:T(1024)S(1)}, u32[]{:S(2)}) copy-start(f32[768]{0:T(1024)S(1)} %convert_element_type.213) | copy-start | bytes 9220
  60.0 18.4 %copy-start.27 = (f32[576]{0:T(1024)}, f32[576]{0:T(1024)S(1)}, u32[]{:S(2)}) copy-start(f32[576]{0:T(1024)S(1)} %broadcast_multiply_fusion.5) | copy-start | bytes 6916
  61.6 16.8 %copy-start.37 = (f32[576]{0:T(1024)}, f32[576]{0:T(1024)S(1)}, u32[]{:S(2)}) copy-start(f32[576]{0:T(1024)S(1)} %add_rsqrt_fusion.1) | copy-start | bytes 6916
  80.1 11.3 %copy-start.1 = (bf16[576,768]{0,1:T(8,128)(2,1)}, bf16[576,768]{0,1:T(8,128)(2,1)S(1)}, u32[]{:S(2)}) copy-start(bf16[576,768]{0,1:T(8,128)(2,1)S(1)} %copy.62) | copy-start | bytes 2654212
  82.0 9.4 %copy-start.3 = (bf16[576,768]{0,1:T(8,128)(2,1)}, bf16[576,768]{0,1:T(8,128)(2,1)S(1)}, u32[]{:S(2)}) copy-start(bf16[576,768]{0,1:T(8,128)(2,1)S(1)} %copy.61) | copy-start | bytes 2654212
  91.4 8.6 %copy-start.12 = (bf16[576,768]{0,1:T(8,128)(2,1)S(1)}, bf16[576,768]{0,1:T(8,128)(2,1)}, u32[]{:S(2)}) copy-start(bf16[576,768]{0,1:T(8,128)(2,1)} %copy.60) | copy-start | bytes 2654212
  100.0 29.4 %copy-start.7 = (bf16[576,768]{1,0:T(8,128)(2,1)S(1)}, bf16[576,768]{1,0:T(8,128)(2,1)}, u32[]{:S(2)}) copy-start(bf16[576,768]{1,0:T(8,128)(2,1)} %param.17) | copy-start | bytes 2654212
  132.3 343.7 %copy-start.26 = (f32[576]{0:T(1024)}, f32[576]{0:T(1024)S(1)}, u32[]{:S(2)}) copy-start(f32[576]{0:T(1024)S(1)} %add_rsqrt_fusion) | copy-start | bytes 6916
  132.7 181.9 %copy-start.5 = (bf16[576,768]{1,0:T(8,128)(2,1)}, bf16[576,768]{1,0:T(8,128)(2,1)S(1)}, u32[]{:S(2)}) copy-start(bf16[576,768]{1,0:T(8,128)(2,1)S(1)} %add_convert_fusion.2) | copy-start | bytes 2654212
  136.2 5.1 copy-start.39
  136.2 5.2 copy-start.43
  136.2 49.0 %all-to-all-start = ((bf16[8,152,768]{2,1,0:T(8,128)(2,1)}), bf16[8,152,768]{2,1,0:T(8,128)(2,1)}, u32[]{:S(2)}, u32[]{:S(2)}) async-start(bf16[8,152,768]{2,1,0:T(8,128)(2,1)} %bitcast.106), calls=%async_computation | async-start | bytes 3735552 | tf_op jit(solution)/shard_map/all_to_all | solution.py:181
  197.9 34.2 %copy-start = (f32[8,152,3072]{2,1,0:T(8,128)}, f32[8,152,3072]{2,1,0:T(8,128)S(1)}, u32[]{:S(2)}) copy-start(f32[8,152,3072]{2,1,0:T(8,128)S(1)} %get-tuple-element.85) | copy-start | bytes 44826628
  232.0 3.1 copy-start.10
  244.6 4.5 copy-start.44
  244.6 70.4 %all-to-all-start.1 = ((bf16[8,152,768]{2,1,0:T(8,128)(2,1)}), bf16[8,152,768]{2,1,0:T(8,128)(2,1)}, u32[]{:S(2)}, u32[]{:S(2)}) async-start(bf16[8,152,768]{2,1,0:T(8,128)(2,1)} %add_convert_fusion), calls=%async_computation.1 | async-start | bytes 3735552 | tf_op jit(solution)/shard_map/all_to_all | solution.py:189
  249.0 305.8 %all-reduce.14.cloned.1.call-start = ((), (), s32[]{:S(2)}) async-start(), calls=%async_computation.10 | async-start | bytes 9437184 | tf_op jit(solution)/shard_map/psum | solution.py:235
  314.9 3.1 copy-start.22
  318.1 5.0 copy-start.15
  323.1 2.2 copy-start.29
  323.1 2.2 copy-start.31
  323.1 56.0 %slice-start = ((s8[7471104]{0:T(1024)(128)(4,1)}), s8[4194304]{0:T(1024)(128)(4,1)S(1)}, s32[]{:S(2)}) async-start(s8[7471104]{0:T(1024)(128)(4,1)} %bitcast.100), calls=%async_computation.12 | async-start | bytes 8388608
  325.3 53.8 %slice-start.1 = ((s8[7471104]{0:T(1024)(128)(4,1)}), s8[3276800]{0:T(1024)(128)(4,1)S(1)}, s32[]{:S(2)}) async-start(s8[7471104]{0:T(1024)(128)(4,1)} %bitcast.100), calls=%async_computation.13 | async-start | bytes 6553600
  377.9 1.3 copy-start.11
  387.4 224.5 %all-gather.10.cloned.1.call-start = ((), (), s32[]{:S(2)}) async-start(), calls=%async_computation.11 | async-start | bytes 23592960 | tf_op jit(solution)/shard_map/all_gather | solution.py:231
  402.6 3.1 copy-start.47
  425.9 46.6 %all-to-all-start.3 = ((bf16[8,152,768]{2,1,0:T(8,128)(2,1)}), bf16[8,152,768]{2,1,0:T(8,128)(2,1)}, u32[]{:S(2)}, u32[]{:S(2)}) async-start(bf16[8,152,768]{2,1,0:T(8,128)(2,1)} %fusion.54), calls=%async_computation.3 | async-start | bytes 3735552 | tf_op jit(solution)/shard_map/all_to_all | solution.py:241
  430.2 277.5 %reduce-scatter.6.cloned.1.call-start = ((), (), s32[]{:S(2)}) async-start(), calls=%async_computation.9 | async-start | bytes 2433024 | tf_op jit(solution)/shard_map/reduce_scatter | solution.py:298
  476.1 1.6 copy-start.16
  476.1 2.0 copy-start.17
  476.1 2.2 copy-start.23
  476.1 2.2 copy-start.30
  476.1 2.2 copy-start.32
  478.3 2.8 copy-start.46
  484.4 4.2 copy-start.24
  488.2 344.3 %reduce-scatter.4.cloned.1.call-start = ((), (), s32[]{:S(2)}) async-start(), calls=%async_computation.8 | async-start | bytes 7299072 | tf_op jit(solution)/shard_map/reduce_scatter | solution.py:297
  504.8 12.5 %copy-start.4 = (bf16[576,768]{0,1:T(8,128)(2,1)S(1)}, bf16[576,768]{0,1:T(8,128)(2,1)}, u32[]{:S(2)}) copy-start(bf16[576,768]{0,1:T(8,128)(2,1)} %copy-done.3) | copy-start | bytes 2654212
  517.3 2.7 copy-start.2
  520.0 11.1 %copy-start.20 = (bf16[12,64,576]{2,1,0:T(8,128)(2,1)}, bf16[12,64,576]{2,1,0:T(8,128)(2,1)S(1)}, u32[]{:S(2)}) copy-start(bf16[12,64,576]{2,1,0:T(8,128)(2,1)S(1)} %multiply_convert_fusion.1) | copy-start | bytes 2654212
  521.7 9.4 %copy-start.13 = (bf16[12,64,576]{2,1,0:T(8,128)(2,1)}, bf16[12,64,576]{2,1,0:T(8,128)(2,1)S(1)}, u32[]{:S(2)}) copy-start(bf16[12,64,576]{2,1,0:T(8,128)(2,1)S(1)} %multiply_convert_fusion.2) | copy-start | bytes 2654212
  521.7 10.3 %copy-start.8 = (bf16[576,768]{1,0:T(8,128)(2,1)S(1)}, bf16[576,768]{1,0:T(8,128)(2,1)}, u32[]{:S(2)}) copy-start(bf16[576,768]{1,0:T(8,128)(2,1)} %param.17) | copy-start | bytes 2654212
  521.7 10.3 %copy-start.28 = (f32[576]{0:T(1024)S(1)}, f32[576]{0:T(1024)}, u32[]{:S(2)}) copy-start(f32[576]{0:T(1024)} %copy-done.27) | copy-start | bytes 6916
  521.7 10.3 %copy-start.36 = (f32[768]{0:T(1024)S(1)}, f32[768]{0:T(1024)}, u32[]{:S(2)}) copy-start(f32[768]{0:T(1024)} %copy-done.35) | copy-start | bytes 9220
  521.7 10.3 %copy-start.38 = (f32[576]{0:T(1024)S(1)}, f32[576]{0:T(1024)}, u32[]{:S(2)}) copy-start(f32[576]{0:T(1024)} %copy-done.37) | copy-start | bytes 6916
  521.7 10.3 %copy-start.42 = (f32[768]{0:T(1024)S(1)}, f32[768]{0:T(1024)}, u32[]{:S(2)}) copy-start(f32[768]{0:T(1024)} %copy-done.41) | copy-start | bytes 9220
  531.1 0.9 copy-start.18
  538.3 1.2 copy-start.6
  538.3 3.3 copy-start.40
  554.8 7.0 copy-start.9
  554.8 7.0 copy-start.14
  554.8 7.0 copy-start.19
  554.8 7.0 copy-start.21
  554.8 7.0 copy-start.45
  561.8 4.1 copy-start.33
  561.8 4.1 copy-start.34
Sparse Core Ops, SparseCore 0:
  10.9 62.7 all-gather.5
  76.6 52.7 all-gather.7
  387.5 91.5 all-reduce.13
  481.1 121.1 all-gather.9
  608.0 99.6 reduce-scatter.5
  713.8 118.5 reduce-scatter.3
